TPU v7x, 32 devices: a whole 2x2x4 slice. The times are simulated.
32 devices in a mesh: groups: 2 (over x), expert: 16 (over z, y, core).
Axes of the slice: x: 2, y: 2, z: 4, core: 2. Of those that a mesh axis runs over, the one named last changes fastest.
Arguments:
- hidden_states: bfloat16 [2, 1024, 2560], P(None, ('groups', 'expert')), parts along dimension 1, may hold values from -6 to 6
- route_ids: int32 [2, 1024, 8], P(None, ('groups', 'expert')), parts along dimension 1, may hold values from 0 to 15, all different within a row; in each aligned block of 32 rows (0 to 31, 32 to 63, ..., all dimensions but the last counted through in order) at most 24 rows name the same one
- route_weights: float32 [2, 1024, 8], P(None, ('groups', 'expert')), parts along dimension 1, may hold values from 0.05 to 1
- gate_proj: bfloat16 [16, 2560, 768], P('expert'), may hold values from -0.125 to 0.125
- up_proj: bfloat16 [16, 2560, 768], P('expert'), may hold values from -0.125 to 0.125
- down_proj: bfloat16 [16, 768, 2560], P('expert'), may hold values from -0.21875 to 0.21875
Outputs:
- moe_output: bfloat16 [2, 1024, 2560], P(None, ('groups', 'expert')), parts along dimension 1
There are 2 independent parts, one for each index of `groups`. A program takes and returns all parts, laid end to end along the dimension named above; an argument that names none is the same for every part. Nothing has to cross between parts.
Inputs may be any that keep to these rules, and one draw needn't show every extreme that they name: `route_ids`: each row names 8 different experts. In each micro-batch, the 32 rows of one device name one expert at most 24 times, and some device names some expert exactly 24 times.
All inputs are finite; a program needn't handle non-finite values.
Results may differ from a plain program's by a relative error of at most 0.0057.
Values may be sent and summed in bfloat16 or wider, within the bound.
A program may use at most 64 MiB of HBM per device.

v0:
```python
import jax
import jax.numpy as jnp
from jax import lax
from jax.sharding import PartitionSpec as P


def expert_rows(received, gate_proj, up_proj, down_proj):
    sources, slot_count, feature_width = received.shape
    stacked = received.reshape(sources * slot_count, feature_width)
    gate_values = jnp.dot(stacked, gate_proj[0], preferred_element_type=jnp.float32)
    up_values = jnp.dot(stacked, up_proj[0], preferred_element_type=jnp.float32)
    hidden = (jax.nn.silu(gate_values) * up_values).astype(jnp.bfloat16)
    result = jnp.dot(hidden, down_proj[0], preferred_element_type=jnp.float32)
    return result.astype(jnp.bfloat16).reshape(sources, slot_count, feature_width)


def slot_index(route_row, experts, capacity):
    row_count, top_count = route_row.shape
    labels = lax.broadcasted_iota(jnp.int32, (row_count, top_count, experts), 2)
    onehot = (route_row[:, :, None] == labels).astype(jnp.int32)
    per_row = jnp.sum(onehot, axis=1)
    before = jnp.cumsum(per_row, axis=0) - per_row
    position = jnp.sum(onehot * before[:, None, :], axis=2)
    return route_row * capacity + position


def on_device(hidden_states, route_ids, route_weights, gate_proj, up_proj, down_proj):
    step_count, row_count, feature_width = hidden_states.shape
    top_count = route_ids.shape[2]
    experts = lax.axis_size("expert") * gate_proj.shape[0]
    capacity = 3 * row_count * top_count // (2 * experts)
    route_slots = []
    outgoing = []
    for step_index in range(step_count):
        targets = slot_index(route_ids[step_index], experts, capacity)
        labels = lax.broadcasted_iota(jnp.int32, (experts * capacity, row_count, top_count), 0)
        selector = jnp.sum((targets[None, :, :] == labels).astype(jnp.int32), axis=2).astype(
            jnp.bfloat16
        )
        packed = jnp.dot(
            selector, hidden_states[step_index], preferred_element_type=jnp.float32
        ).astype(jnp.bfloat16)
        outgoing.append(packed.reshape(experts, capacity, feature_width))
        route_slots.append(targets)

    def serve_one(received):
        return lax.all_to_all(
            expert_rows(received, gate_proj, up_proj, down_proj),
            "expert",
            split_axis=0,
            concat_axis=0,
            tiled=True,
        )

    returned = [
        serve_one(lax.all_to_all(packed, "expert", split_axis=0, concat_axis=0, tiled=True))
        for packed in outgoing
    ]
    outputs = []
    for step_index in range(step_count):
        weights = route_weights[step_index]
        normalized = weights / jnp.sum(weights, axis=1, keepdims=True)
        returned_rows = returned[step_index].reshape(experts * capacity, feature_width)
        gathered = jnp.take(returned_rows, route_slots[step_index], axis=0)
        combined = jnp.sum(gathered.astype(jnp.float32) * normalized[:, :, None], axis=1)
        outputs.append(combined.astype(jnp.bfloat16))
    return jnp.stack(outputs)


def solution(mesh):
    placed = (
        P(None, ("groups", "expert"), None),
        P(None, ("groups", "expert"), None),
        P(None, ("groups", "expert"), None),
        P("expert", None, None),
        P("expert", None, None),
        P("expert", None, None),
    )
    return jax.shard_map(
        on_device,
        mesh=mesh,
        in_specs=placed,
        out_specs=P(None, ("groups", "expert"), None),
        check_vma=False,
    )
```

profile of v0, /device:TPU:15, one launch (start us, length us, event | category | flops | bytes accessed | tf_op | source)
XLA Modules:
  0.0 212.4 jit_solution(2939662833502115000)
XLA Ops:
  0.0 0.7 slice_bitcast_fusion.1
  0.7 0.1 copy.25
  0.8 0.1 reduce_window_sum.17
  0.8 0.1 copy.27
  1.0 0.7 fusion.35
  1.7 0.1 copy.29
  1.7 0.2 convert_reduce_fusion.1
  1.9 2.9 %convolution_convert_fusion.3 = bf16[384,2560]{1,0:T(8,128)(2,1)} fusion(bf16[2,32,2560]{2,1,0:T(8,128)(2,1)} %param.8, s32[384,32]{0,1:T(8,128)S(1)} %convert_reduce_fusion.1), kind=kOutput, calls=%fused_computation.5 | convolution fusion | flops 63909888 | bytes 2179072 | tf_op jit(solution)/shard_map/dot_general | solution.py:40
  4.8 0.0 copy-start.1
  4.8 0.0 copy-start
  4.8 6.7 %all-to-all-start = ((bf16[16,24,2560]{2,1,0:T(8,128)(2,1)}), bf16[16,24,2560]{2,1,0:T(8,128)(2,1)S(1)}, u32[]{:S(2)}, u32[]{:S(2)}) async-start(bf16[16,24,2560]{2,1,0:T(8,128)(2,1)} %bitcast.4), calls=%async_computation | async-start | bytes 3932160 | tf_op jit(solution)/shard_map/all_to_all | solution.py:56
  11.5 0.1 copy.32
  11.6 0.1 reduce_window_sum.18
  11.6 0.1 copy.34
  11.7 0.0 copy-done.1
  11.8 0.1 copy.36
  11.8 0.2 convert_reduce_fusion
  12.0 0.0 copy-done
  12.0 2.0 convolution_convert_fusion.1
  14.0 42.1 %all-to-all-done = bf16[16,24,2560]{2,1,0:T(8,128)(2,1)S(1)} async-done(((bf16[16,24,2560]{2,1,0:T(8,128)(2,1)}), bf16[16,24,2560]{2,1,0:T(8,128)(2,1)S(1)}, u32[]{:S(2)}, u32[]{:S(2)}) %all-to-all-start) | async-done | bytes 1966112 | tf_op jit(solution)/shard_map/all_to_all | solution.py:56
  56.1 4.8 %all-to-all-start.2 = ((bf16[16,24,2560]{2,1,0:T(8,128)(2,1)}), bf16[16,24,2560]{2,1,0:T(8,128)(2,1)}, u32[]{:S(2)}, u32[]{:S(2)}) async-start(bf16[16,24,2560]{2,1,0:T(8,128)(2,1)} %bitcast.18), calls=%async_computation.2 | async-start | bytes 3932160 | tf_op jit(solution)/shard_map/all_to_all | solution.py:56
  60.9 3.8 %fusion.8 = f32[384,768]{1,0:T(8,128)S(1)} fusion(bf16[384,2560]{1,0:T(8,128)(2,1)S(1)} %bitcast.87, bf16[1,2560,768]{2,1,0:T(8,128)(2,1)} %param.11), kind=kOutput, calls=%fused_computation.14 | convolution fusion | flops 1509949440 | bytes 7077888 | tf_op jit(solution)/shard_map/dot_general | solution.py:10
  64.7 8.9 %convolution_convert_fusion.2 = bf16[384,2560]{1,0:T(8,128)(2,1)} fusion(bf16[1,768,2560]{2,1,0:T(8,128)(2,1)} %param.13, bf16[384,2560]{1,0:T(8,128)(2,1)S(1)} %bitcast.88, bf16[1,2560,768]{2,1,0:T(8,128)(2,1)} %param.12, f32[384,768]{1,0:T(8,128)S(1)} %fusion.8), kind=kOutput, calls=%fused_computation.4 | convolution fusion | flops 3022651392 | bytes 12976128 | tf_op jit(solution)/shard_map/dot_general | solution.py:13
  73.5 32.1 %all-to-all-done.2 = bf16[16,24,2560]{2,1,0:T(8,128)(2,1)} async-done(((bf16[16,24,2560]{2,1,0:T(8,128)(2,1)}), bf16[16,24,2560]{2,1,0:T(8,128)(2,1)}, u32[]{:S(2)}, u32[]{:S(2)}) %all-to-all-start.2) | async-done | bytes 1966112 | tf_op jit(solution)/shard_map/all_to_all | solution.py:56
  105.6 4.8 %all-to-all-start.1 = ((bf16[16,24,2560]{2,1,0:T(8,128)(2,1)}), bf16[16,24,2560]{2,1,0:T(8,128)(2,1)S(1)}, u32[]{:S(2)}, u32[]{:S(2)}) async-start(bf16[16,24,2560]{2,1,0:T(8,128)(2,1)} %bitcast.89), calls=%async_computation.1 | async-start | bytes 3932160 | tf_op jit(solution)/shard_map/all_to_all | solution.py:47
  110.4 4.4 %fusion.6 = f32[384,768]{1,0:T(8,128)S(1)} fusion(bf16[384,2560]{1,0:T(8,128)(2,1)} %bitcast.19, bf16[1,2560,768]{2,1,0:T(8,128)(2,1)} %param.11), kind=kOutput, calls=%fused_computation.12 | convolution fusion | flops 1509949440 | bytes 7077888 | tf_op jit(solution)/shard_map/dot_general | solution.py:10
  114.8 9.4 %convolution_convert_fusion = bf16[384,2560]{1,0:T(8,128)(2,1)} fusion(bf16[1,768,2560]{2,1,0:T(8,128)(2,1)} %param.13, bf16[384,2560]{1,0:T(8,128)(2,1)} %bitcast.19, bf16[1,2560,768]{2,1,0:T(8,128)(2,1)} %param.12, f32[384,768]{1,0:T(8,128)S(1)} %fusion.6), kind=kOutput, calls=%fused_computation.2 | convolution fusion | flops 3022651392 | bytes 12976128 | tf_op jit(solution)/shard_map/dot_general | solution.py:13
  124.2 30.8 %all-to-all-done.1 = bf16[16,24,2560]{2,1,0:T(8,128)(2,1)S(1)} async-done(((bf16[16,24,2560]{2,1,0:T(8,128)(2,1)}), bf16[16,24,2560]{2,1,0:T(8,128)(2,1)S(1)}, u32[]{:S(2)}, u32[]{:S(2)}) %all-to-all-start.1) | async-done | bytes 1966112 | tf_op jit(solution)/shard_map/all_to_all | solution.py:47
  155.0 0.0 copy-start.2
  155.0 4.9 %all-to-all-start.3 = ((bf16[16,24,2560]{2,1,0:T(8,128)(2,1)}), bf16[16,24,2560]{2,1,0:T(8,128)(2,1)}, u32[]{:S(2)}, u32[]{:S(2)}) async-start(bf16[16,24,2560]{2,1,0:T(8,128)(2,1)} %bitcast.86), calls=%async_computation.3 | async-start | bytes 3932160 | tf_op jit(solution)/shard_map/all_to_all | solution.py:47
  159.9 0.1 copy.30
  160.0 0.1 reshape.135
  160.1 0.1 copy.28
  160.2 0.0 copy-done.2
  160.2 0.1 copy.31
  160.3 0.1 copy.37
  160.4 0.1 reshape.139
  160.5 0.1 copy.35
  160.5 0.1 copy.38
  160.6 1.4 gather_fusion
  162.1 42.5 %all-to-all-done.3 = bf16[16,24,2560]{2,1,0:T(8,128)(2,1)} async-done(((bf16[16,24,2560]{2,1,0:T(8,128)(2,1)}), bf16[16,24,2560]{2,1,0:T(8,128)(2,1)}, u32[]{:S(2)}, u32[]{:S(2)}) %all-to-all-start.3) | async-done | bytes 1966112 | tf_op jit(solution)/shard_map/all_to_all | solution.py:47
  204.6 4.5 %gather_fusion.1 = bf16[256,2560]{1,0:T(8,128)(2,1)S(1)} fusion(bf16[384,2560]{1,0:T(8,128)(2,1)} %bitcast.21, s32[1024]{0:T(1024)S(1)} %pad_clamp_fusion), kind=kCustom, calls=%fused_computation.1.clone | custom fusion | bytes 2622464 | tf_op jit(solution)/shard_map/jit(_take)/gather | solution.py:64
  209.1 1.3 multiply_reduce_fusion.1
  210.4 1.3 multiply_reduce_fusion
  211.7 0.8 pad_maximum_fusion
  (12 shorter events, 0.2 us)
Async XLA Ops:
  4.8 6.9 %copy-start.1 = (s32[2,32,8]{1,2,0:T(8,128)S(1)}, s32[2,32,8]{1,2,0:T(8,128)}, u32[]{:S(2)}) copy-start(s32[2,32,8]{1,2,0:T(8,128)} %param.9) | copy-start | bytes 6148
  4.8 7.2 %copy-start = (bf16[2,32,2560]{2,1,0:T(8,128)(2,1)S(1)}, bf16[2,32,2560]{2,1,0:T(8,128)(2,1)}, u32[]{:S(2)}) copy-start(bf16[2,32,2560]{2,1,0:T(8,128)(2,1)} %param.8) | copy-start | bytes 983044
  4.8 51.3 %all-to-all-start = ((bf16[16,24,2560]{2,1,0:T(8,128)(2,1)}), bf16[16,24,2560]{2,1,0:T(8,128)(2,1)S(1)}, u32[]{:S(2)}, u32[]{:S(2)}) async-start(bf16[16,24,2560]{2,1,0:T(8,128)(2,1)} %bitcast.4), calls=%async_computation | async-start | bytes 3932160 | tf_op jit(solution)/shard_map/all_to_all | solution.py:56
  56.1 49.5 %all-to-all-start.2 = ((bf16[16,24,2560]{2,1,0:T(8,128)(2,1)}), bf16[16,24,2560]{2,1,0:T(8,128)(2,1)}, u32[]{:S(2)}, u32[]{:S(2)}) async-start(bf16[16,24,2560]{2,1,0:T(8,128)(2,1)} %bitcast.18), calls=%async_computation.2 | async-start | bytes 3932160 | tf_op jit(solution)/shard_map/all_to_all | solution.py:56
  105.6 49.4 %all-to-all-start.1 = ((bf16[16,24,2560]{2,1,0:T(8,128)(2,1)}), bf16[16,24,2560]{2,1,0:T(8,128)(2,1)S(1)}, u32[]{:S(2)}, u32[]{:S(2)}) async-start(bf16[16,24,2560]{2,1,0:T(8,128)(2,1)} %bitcast.89), calls=%async_computation.1 | async-start | bytes 3932160 | tf_op jit(solution)/shard_map/all_to_all | solution.py:47
  155.0 5.2 %copy-start.2 = (f32[2,32,8]{1,2,0:T(8,128)S(1)}, f32[2,32,8]{1,2,0:T(8,128)}, u32[]{:S(2)}) copy-start(f32[2,32,8]{1,2,0:T(8,128)} %param.10) | copy-start | bytes 6148
  155.0 49.6 %all-to-all-start.3 = ((bf16[16,24,2560]{2,1,0:T(8,128)(2,1)}), bf16[16,24,2560]{2,1,0:T(8,128)(2,1)}, u32[]{:S(2)}, u32[]{:S(2)}) async-start(bf16[16,24,2560]{2,1,0:T(8,128)(2,1)} %bitcast.86), calls=%async_computation.3 | async-start | bytes 3932160 | tf_op jit(solution)/shard_map/all_to_all | solution.py:47
where the time goes:
time: 213 us; the launch traced here: 212 us
  waiting for transfers between devices  147 us (69%)
  matrix products  31.3 us (15%)
  starting transfers between devices  21.1 us (10%)
  local copies, waits for them, and re-layouts  7.79 us (4%)
  other arithmetic  4.6 us (2%)
    all_to_all x2, waiting for transfers between devices, on_device(): lax.all_to_all(packed, 'expert', split_axis=0, concat_axis=0, tiled=True)  74.1 us
    all_to_all x2, waiting for transfers between devices, serve_one(): lax.all_to_all(expert_rows(received, gate_proj, up_proj, down_proj), 'exp...  73.3 us
    dot_general x2, matrix products, expert_rows(): result = jnp.dot(hidden, down_proj[0], preferred_element_type=jnp.float32)  18.3 us
    all_to_all x2, starting transfers between devices, on_device(): lax.all_to_all(packed, 'expert', split_axis=0, concat_axis=0, tiled=True)  11.4 us
    all_to_all x2, starting transfers between devices, serve_one(): lax.all_to_all(expert_rows(received, gate_proj, up_proj, down_proj), 'exp...  9.69 us
    dot_general x2, matrix products, expert_rows(): jnp.dot(stacked, gate_proj[0], preferred_element_type=jnp.float32)  8.18 us
    gather x2, local copies, waits for them, and re-layouts, on_device(): gathered = jnp.take(returned_rows, route_slots[step_index], axis=0)  5.98 us
    dot_general x2, matrix products, on_device(): jnp.dot(selector, hidden_states[step_index], preferred_element_type=jnp.f...  4.87 us
  transfers between devices with their start and end apart: 4, of which 4 were waited for; matrix products, arithmetic and copies ran while one was open for 15% of the time, Pallas kernels for 0%

commit v1 on v0

v1 whole, which is shorter than its diff:
```python
import jax
import jax.numpy as jnp
from jax import lax
from jax.sharding import PartitionSpec as P


def on_device(hidden_states, route_ids, route_weights, gate_proj, up_proj, down_proj):
    step_count, row_count, feature_width = hidden_states.shape
    experts = lax.axis_size("expert")
    me = lax.axis_index("expert")
    normalized = route_weights / jnp.sum(route_weights, axis=2, keepdims=True)
    labels = lax.broadcasted_iota(jnp.int32, (1, 1, 1, experts), 3)
    dense = jnp.sum(
        jnp.where(route_ids[:, :, :, None] == labels, normalized[:, :, :, None], 0.0), axis=2
    )
    all_dense = lax.all_gather(dense, "expert", axis=1, tiled=True)
    mine = jnp.sum(
        jnp.where(lax.broadcasted_iota(jnp.int32, (1, 1, experts), 2) == me, all_dense, 0.0),
        axis=2,
    )
    outputs = []
    for step in range(step_count):
        tokens = lax.all_gather(hidden_states[step], "expert", axis=0, tiled=True)
        gate_values = jnp.dot(tokens, gate_proj[0], preferred_element_type=jnp.float32)
        up_values = jnp.dot(tokens, up_proj[0], preferred_element_type=jnp.float32)
        hidden = (jax.nn.silu(gate_values) * up_values).astype(jnp.bfloat16)
        result = jnp.dot(hidden, down_proj[0], preferred_element_type=jnp.float32)
        partial = (result * mine[step][:, None]).astype(jnp.bfloat16)
        outputs.append(lax.psum_scatter(partial, "expert", scatter_dimension=0, tiled=True))
    return jnp.stack(outputs)


def solution(mesh):
    placed = (
        P(None, ("groups", "expert"), None),
        P(None, ("groups", "expert"), None),
        P(None, ("groups", "expert"), None),
        P("expert", None, None),
        P("expert", None, None),
        P("expert", None, None),
    )
    return jax.shard_map(
        on_device,
        mesh=mesh,
        in_specs=placed,
        out_specs=P(None, ("groups", "expert"), None),
        check_vma=False,
    )
```

time: 213 us -> 242 us (1.14)
  the two profiles are of different devices: /device:TPU:15 before, /device:TPU:0 now
where the time goes in v1:
time: 242 us
  waiting for transfers between devices  162 us (67%)
  matrix products  35.1 us (15%)
  blocking collectives  25.4 us (10%)
  between operations  13.1 us (5%)
  other arithmetic  3.89 us (2%)
    reduce_scatter x2, waiting for transfers between devices, on_device(): lax.psum_scatter(partial, 'expert', scatter_dimension=0, tiled=True)  116 us
    all_gather x2, waiting for transfers between devices, on_device(): tokens = lax.all_gather(hidden_states[step], 'expert', axis=0, tiled=True)  45.5 us
    all_gather x1, blocking collectives, on_device(): all_dense = lax.all_gather(dense, 'expert', axis=1, tiled=True)  25.4 us
    dot_general x2, matrix products, on_device(): result = jnp.dot(hidden, down_proj[0], preferred_element_type=jnp.float32)  22.1 us
    dot_general x2, matrix products, on_device(): jnp.dot(tokens, gate_proj[0], preferred_element_type=jnp.float32)  12.9 us
  transfers between devices with their start and end apart: 4, of which 4 were waited for; matrix products, arithmetic and copies ran while one was open for 16% of the time, Pallas kernels for 0%

profile of v1, /device:TPU:0, one launch (start us, length us, event | category | flops | bytes accessed | tf_op | source)
XLA Modules:
  0.0 242.1 jit_solution(13985437218307566842)
XLA Ops:
  6.5 0.0 all-gather.5.cloned.1.call-start
  6.5 1.7 fusion.36
  8.3 0.0 all-gather.5.cloned.1.call-update
  8.3 0.0 all-gather.7.cloned.1.call-start
  8.3 0.7 all-gather.7.cloned.1.call-update
  9.0 0.0 reduce-scatter.3.cloned.1.call-start
  9.1 0.8 fusion.33
  9.9 0.7 select_reduce_fusion.1
  10.6 0.1 copy.9
  10.7 25.4 %all_gather.10 = f32[2,512,16]{2,0,1:T(2,128)S(1)} all-gather(f32[2,32,16]{2,0,1:T(2,128)S(1)} %copy.9), channel_id=1, replica_groups=mesh['groups'=2,'expert'=16] {'expert'}, dimensions={1}, use_global_device_ids=true | all-gather | bytes 69632 | tf_op jit(solution)/shard_map/all_gather | solution.py:16
  36.1 0.6 select_reduce_fusion
  36.7 0.1 fusion.37
  36.9 0.1 copy.12
  37.0 18.9 %all-gather.5.cloned.1.call-done = bf16[1,512,2560]{2,1,0:T(8,128)(2,1)} async-done(((bf16[1,32,2560]{2,1,0:T(8,128)(2,1)}), bf16[1,512,2560]{2,1,0:T(8,128)(2,1)}) %all-gather.5.cloned.1.call-update) | async-done | bytes 2621456 | tf_op jit(solution)/shard_map/all_gather | solution.py:23
  55.9 0.0 copy-start.1
  55.9 6.5 %fusion.8 = f32[512,768]{1,0:T(8,128)} fusion(bf16[1,2560,768]{2,1,0:T(8,128)(2,1)} %param.9, bf16[1,512,2560]{2,1,0:T(8,128)(2,1)} %all-gather.5.cloned.1.call-done), kind=kOutput, calls=%fused_computation.10 | convolution fusion | flops 2013265920 | bytes 8126464 | tf_op jit(solution)/shard_map/dot_general | solution.py:24
  62.4 0.0 copy-done.1
  62.4 11.0 %multiply_convert_fusion.1 = bf16[512,2560]{1,0:T(8,128)(2,1)} fusion(bf16[1,768,2560]{2,1,0:T(8,128)(2,1)} %param.11, f32[512]{0:T(512)S(1)} %bitcast.48, f32[512,768]{1,0:T(8,128)} %fusion.8, bf16[1,2560,768]{2,1,0:T(8,128)(2,1)} %param.10, bf16[1,512,2560]{2,1,0:T(8,128)(2,1)S(1)} %copy-done.1), kind=kOutput, calls=%fused_computation.1 | convolution fusion | flops 4031512576 | bytes 14682112 | tf_op jit(solution)/shard_map/dot_general | solution.py:27
  73.4 0.0 reduce-scatter.3.cloned.1.call-update
  73.5 0.0 reduce-scatter.5.cloned.1.call-start
  73.5 0.1 copy.13
  73.6 26.5 %all-gather.7.cloned.1.call-done = bf16[1,512,2560]{2,1,0:T(8,128)(2,1)} async-done(((bf16[1,32,2560]{2,1,0:T(8,128)(2,1)}), bf16[1,512,2560]{2,1,0:T(8,128)(2,1)}) %all-gather.7.cloned.1.call-update) | async-done | bytes 2621456 | tf_op jit(solution)/shard_map/all_gather | solution.py:23
  100.2 0.0 copy-start
  100.2 6.5 %fusion.6 = f32[512,768]{1,0:T(8,128)} fusion(bf16[1,2560,768]{2,1,0:T(8,128)(2,1)} %param.9, bf16[1,512,2560]{2,1,0:T(8,128)(2,1)} %all-gather.7.cloned.1.call-done), kind=kOutput, calls=%fused_computation.8 | convolution fusion | flops 2013265920 | bytes 8126464 | tf_op jit(solution)/shard_map/dot_general | solution.py:24
  106.6 0.0 copy-done
  106.6 11.1 %multiply_convert_fusion = bf16[512,2560]{1,0:T(8,128)(2,1)} fusion(bf16[1,768,2560]{2,1,0:T(8,128)(2,1)} %param.11, f32[512]{0:T(512)S(1)} %bitcast.49, f32[512,768]{1,0:T(8,128)} %fusion.6, bf16[1,2560,768]{2,1,0:T(8,128)(2,1)} %param.10, bf16[1,512,2560]{2,1,0:T(8,128)(2,1)S(1)} %copy-done), kind=kOutput, calls=%fused_computation | convolution fusion | flops 4031512576 | bytes 14682112 | tf_op jit(solution)/shard_map/dot_general | solution.py:27
  117.7 0.0 reduce-scatter.5.cloned.1.call-update
  117.8 49.2 %reduce-scatter.3.cloned.1.call-done = bf16[32,2560]{1,0:T(8,128)(2,1)} async-done(((bf16[512,2560]{1,0:T(8,128)(2,1)}), bf16[32,2560]{1,0:T(8,128)(2,1)}) %reduce-scatter.3.cloned.1.call-update) | async-done | bytes 163856 | tf_op jit(solution)/shard_map/reduce_scatter | solution.py:29
  167.0 66.8 %reduce-scatter.5.cloned.1.call-done = bf16[32,2560]{1,0:T(8,128)(2,1)} async-done(((bf16[512,2560]{1,0:T(8,128)(2,1)}), bf16[32,2560]{1,0:T(8,128)(2,1)}) %reduce-scatter.5.cloned.1.call-update) | async-done | bytes 163856 | tf_op jit(solution)/shard_map/reduce_scatter | solution.py:29
  233.9 1.7 pad_maximum_fusion
  (1 shorter events, 0.0 us)
Async XLA Ops:
  6.5 49.4 %all-gather.5.cloned.1.call-start = ((), (), s32[]{:S(2)}) async-start(), calls=%async_computation.4 | async-start | bytes 2785280 | tf_op jit(solution)/shard_map/all_gather | solution.py:23
  8.3 91.9 %all-gather.7.cloned.1.call-start = ((), (), s32[]{:S(2)}) async-start(), calls=%async_computation.5 | async-start | bytes 2785280 | tf_op jit(solution)/shard_map/all_gather | solution.py:23
  9.0 158.0 %reduce-scatter.3.cloned.1.call-start = ((), (), s32[]{:S(2)}) async-start(), calls=%async_computation.2 | async-start | bytes 2785280 | tf_op jit(solution)/shard_map/reduce_scatter | solution.py:29
  55.9 6.5 %copy-start.1 = (bf16[1,512,2560]{2,1,0:T(8,128)(2,1)S(1)}, bf16[1,512,2560]{2,1,0:T(8,128)(2,1)}, u32[]{:S(2)}) copy-start(bf16[1,512,2560]{2,1,0:T(8,128)(2,1)} %all-gather.5.cloned.1.call-done) | copy-start | bytes 7864324
  73.5 160.4 %reduce-scatter.5.cloned.1.call-start = ((), (), s32[]{:S(2)}) async-start(), calls=%async_computation.3 | async-start | bytes 2785280 | tf_op jit(solution)/shard_map/reduce_scatter | solution.py:29
  100.2 6.5 %copy-start = (bf16[1,512,2560]{2,1,0:T(8,128)(2,1)S(1)}, bf16[1,512,2560]{2,1,0:T(8,128)(2,1)}, u32[]{:S(2)}) copy-start(bf16[1,512,2560]{2,1,0:T(8,128)(2,1)} %all-gather.7.cloned.1.call-done) | copy-start | bytes 7864324
Sparse Core Ops, SparseCore 0:
  9.6 46.2 all-gather.4
  58.2 41.8 all-gather.6
  103.9 63.0 reduce-scatter.2
  170.6 63.1 reduce-scatter.4

commit v2 on v1

v2 whole, which is shorter than its diff:
```python
import functools

import jax
import jax.numpy as jnp
from jax import lax
from jax.experimental import pallas as pl
from jax.experimental.pallas import tpu as pltpu
from jax.sharding import PartitionSpec as P

MESH = pl.DeviceIdType.MESH
LANES = 128


def kernel(
    chips,
    across,
    hidden_ref,
    ids_ref,
    weights_ref,
    gate_hbm,
    up_hbm,
    down_hbm,
    out_ref,
    x,
    pc,
    rs,
    gate,
    up,
    down,
    mid,
    load_sem,
    ag_s,
    ag_r,
    pf_s,
    pf_r,
    pc_s,
    pc_r,
    rs_s,
    rs_r,
):
    steps, _, _, rows, _ = x.shape
    width = out_ref.shape[2]
    inner = gate.shape[1]
    experts = 2 * chips
    hops = (chips // 2, chips - 1 - chips // 2)
    along = chips // across

    me = lax.axis_index("expert")
    core = lax.rem(me, 2)
    chip = lax.div(me, 2)
    if across == 2:
        far, deep = lax.rem(chip, 2), lax.div(chip, 2)
        here = (1 - far) * deep + far * (2 * along - 1 - deep)
    else:
        here = chip

    def device_at(position):
        if across == 2:
            far = lax.div(position, along)
            deep = (1 - far) * position + far * (2 * along - 1 - position)
            position = deep * 2 + far
        return {"expert": position * 2 + core}

    sign = 1 - 2 * core
    neighbours = (
        device_at(lax.rem(here + sign + chips, chips)),
        device_at(lax.rem(here - sign + chips, chips)),
    )
    partner = {"expert": chip * 2 + (1 - core)}

    def slot(direction, hop):
        return hop if direction == 0 else (chips - hop) % chips

    order = [0]
    for hop in range(1, chips // 2 + 1):
        order += [slot(d, hop) for d in range(2) if hop <= hops[d]]
    place = {s: i for i, s in enumerate(order)}
    values = pl.ds(0, width)

    def remote(src, dst, send, recv, target):
        return pltpu.make_async_remote_copy(
            src_ref=src,
            dst_ref=dst,
            send_sem=send,
            recv_sem=recv,
            device_id=target,
            device_id_type=MESH,
        )

    def mirror(s):
        return (chips - s) % chips

    def ag_copy(st, d, hop):
        return remote(
            x.at[st, place[slot(d, hop - 1)], 0],
            x.at[st, place[slot(d, hop)], 0],
            ag_s.at[st, d, hop - 1],
            ag_r.at[st, d, hop - 1],
            neighbours[d],
        )

    def pf_copy(st, s):
        return remote(
            x.at[st, place[s], 0],
            x.at[st, place[mirror(s)], 1],
            pf_s.at[st, s],
            pf_r.at[st, mirror(s)],
            partner,
        )

    def pc_copy(st, s):
        return remote(
            x.at[st, place[s], 1, :, values],
            pc.at[st, mirror(s)],
            pc_s.at[st, s],
            pc_r.at[st, mirror(s)],
            partner,
        )

    def rs_copy(st, d, hop):
        target = slot(d, hop - 1) if (d == 0 or hop > 1) else chips // 2
        return remote(
            x.at[st, place[slot(d, hop)], 0, :, values],
            rs.at[st, target],
            rs_s.at[st, d, hop - 1],
            rs_r.at[st, d, hop - 1],
            neighbours[1 - d],
        )

    own = [
        pltpu.make_async_copy(
            hidden_ref.at[st], x.at[st, 0, 0, :, values], load_sem.at[3 + st]
        )
        for st in range(steps)
    ]
    for copy in own:
        copy.start()
    loads = [
        pltpu.make_async_copy(src.at[0], dst, load_sem.at[i])
        for i, (src, dst) in enumerate(((gate_hbm, gate), (up_hbm, up), (down_hbm, down)))
    ]
    for copy in loads:
        copy.start()

    barrier = pltpu.get_barrier_semaphore()
    for target in (*neighbours, partner):
        pl.semaphore_signal(barrier, inc=1, device_id=target, device_id_type=MESH)

    extra = x.shape[4] - width
    lane = lax.broadcasted_iota(jnp.int32, (rows, extra), 1)
    for st in range(steps):
        raw = weights_ref[st]
        normalized = raw / jnp.sum(raw, axis=1, keepdims=True)
        ids = ids_ref[st]
        dense = jnp.zeros((rows, extra), jnp.float32)
        for k in range(ids.shape[1]):
            label = ids[:, k : k + 1]
            hit = (lane == label) | (lane == label + experts)
            dense = dense + jnp.where(hit, normalized[:, k : k + 1], 0.0)
        high = dense.astype(jnp.bfloat16).astype(jnp.float32)
        low = dense - high
        x[st, 0, 0, :, pl.ds(width, extra)] = jnp.where(lane < experts, high, low).astype(
            jnp.bfloat16
        )
    pl.semaphore_wait(barrier, 3)

    def ag_open(st):
        own[st].wait()
        for d in range(2):
            ag_copy(st, d, 1).start()
        pf_copy(st, 0).start()

    def ag_event(st, hop):
        for d in range(2):
            if hop <= hops[d]:
                ag_copy(st, d, hop).wait_recv()
                if hop < hops[d]:
                    ag_copy(st, d, hop + 1).start()
                pf_copy(st, slot(d, hop)).start()

    def total(st, s, received):
        value = x[st, place[s], 0, :, values].astype(jnp.float32)
        value = value + pc[st, s].astype(jnp.float32)
        for index in received:
            value = value + rs[st, index].astype(jnp.float32)
        return value.astype(jnp.bfloat16)

    def rs_event(st, hop):
        for d in range(2):
            if hop <= hops[d]:
                s = slot(d, hop)
                received = []
                if hop < hops[d]:
                    rs_copy(st, d, hop + 1).wait_recv()
                    received = [s]
                pc_copy(st, mirror(s)).wait_recv()
                x[st, place[s], 0, :, values] = total(st, s, received)
                rs_copy(st, d, hop).start()

    def rs_close(st):
        for d in range(2):
            rs_copy(st, d, 1).wait_recv()
        pc_copy(st, 0).wait_recv()
        out_ref[st] = total(st, 0, [0, chips // 2])

    group = chips // 2
    block = min(4, group)
    tall = block * 2 * rows
    ff_tile = 256 if inner % 256 == 0 else inner
    out_tile = 512 if width % 512 == 0 else width

    def over_blocks(first, body):
        if group == block:
            body(first, 0)
        else:
            def step(i, carry):
                body(first + i * block, i * tall)
                return carry

            lax.fori_loop(0, group // block, step, 0)

    def gate_up(st, part, tile):
        columns = pl.ds(tile * ff_tile, ff_tile)

        def body(first, row):
            rows_in = x[st, pl.ds(first, block), :, :, values].reshape(tall, width)
            g = jnp.dot(rows_in, gate[:, columns], preferred_element_type=jnp.float32)
            u = jnp.dot(rows_in, up[:, columns], preferred_element_type=jnp.float32)
            mid[pl.ds(row, tall), columns] = (g / (1.0 + jnp.exp(-g)) * u).astype(jnp.bfloat16)

        over_blocks(part * group, body)

    def down_all(st, part):
        for s in order[part * group : (part + 1) * group]:
            pf_copy(st, s).wait_send()
            for d in range(2):
                for hop in range(hops[d]):
                    if slot(d, hop) == s:
                        ag_copy(st, d, hop + 1).wait_send()

        def body(first, row):
            marks = x[st, pl.ds(first, block), :, :, pl.ds(width, extra)].reshape(tall, extra)
            spot = lax.broadcasted_iota(jnp.int32, (tall, extra), 1)
            picked = (spot == me) | (spot == me + experts)
            scale = jnp.sum(
                jnp.where(picked, marks.astype(jnp.float32), 0.0), axis=1, keepdims=True
            )
            rows_in = mid[pl.ds(row, tall), :]

            def tile(i, carry):
                columns = pl.ds(pl.multiple_of(i * out_tile, out_tile), out_tile)
                y = jnp.dot(rows_in, down[:, columns], preferred_element_type=jnp.float32)
                y = (y * scale).astype(jnp.bfloat16).reshape(block, 2, rows, out_tile)
                x[st, pl.ds(first, block), :, :, columns] = y
                return carry

            lax.fori_loop(0, width // out_tile, tile, 0)

        over_blocks(part * group, body)
        for s in order[part * group : (part + 1) * group]:
            pc_copy(st, s).start()

    def arrive(st, part):
        for s in order[part * group : (part + 1) * group]:
            pf_copy(st, mirror(s)).wait_recv()

    def compute(st, part, events):
        tiles = inner // ff_tile
        pieces = tiles + 1
        arrive(st, part)
        taken = 0
        for piece in range(pieces):
            if piece < tiles:
                gate_up(st, part, piece)
            else:
                down_all(st, part)
            until = (piece + 1) * len(events) // pieces
            for event in events[taken:until]:
                event()
            taken = until

    near = group // 2
    call = functools.partial
    ag_open(0)
    for hop in range(1, near + 1):
        ag_event(0, hop)
    for copy in loads:
        copy.wait()
    rest = [call(ag_event, 0, hop) for hop in range(near + 1, hops[0] + 1)]
    compute(0, 0, rest + [call(ag_open, 1)])
    later = [call(ag_event, 1, hop) for hop in range(1, hops[0] + 1)]
    compute(0, 1, later[:near])
    back = [call(rs_event, 0, hop) for hop in range(hops[0], 0, -1)]
    mixed = []
    for i in range(near):
        mixed += [back[i]] + later[near + i * (len(later) - near) // near : near + (i + 1) * (len(later) - near) // near]
    compute(1, 0, mixed)
    compute(1, 1, back[near:] + [call(rs_close, 0)])
    for hop in range(hops[0], 0, -1):
        rs_event(1, hop)
    rs_close(1)

    for st in range(steps):
        for d in range(2):
            for hop in range(1, hops[d] + 1):
                rs_copy(st, d, hop).wait_send()
        for s in range(chips):
            pc_copy(st, s).wait_send()


def on_device(across, hidden_states, route_ids, route_weights, gate_proj, up_proj, down_proj):
    steps, rows, width = hidden_states.shape
    experts = lax.axis_size("expert")
    inner = gate_proj.shape[2]
    chips = experts // 2
    hops = chips // 2
    extra = -(-2 * experts // LANES) * LANES
    dma = pltpu.SemaphoreType.DMA
    bf16 = jnp.bfloat16
    vmem = pl.BlockSpec(memory_space=pltpu.VMEM)
    hbm = pl.BlockSpec(memory_space=pl.ANY)
    return pl.pallas_call(
        functools.partial(kernel, chips, across),
        out_shape=jax.ShapeDtypeStruct((steps, rows, width), bf16),
        in_specs=[hbm, vmem, vmem, hbm, hbm, hbm],
        out_specs=vmem,
        scratch_shapes=[
            pltpu.VMEM((steps, chips, 2, rows, width + extra), bf16),
            pltpu.VMEM((steps, chips, rows, width), bf16),
            pltpu.VMEM((steps, chips, rows, width), bf16),
            pltpu.VMEM((width, inner), bf16),
            pltpu.VMEM((width, inner), bf16),
            pltpu.VMEM((inner, width), bf16),
            pltpu.VMEM((chips * rows, inner), bf16),
            dma((3 + steps,)),
            dma((steps, 2, hops)),
            dma((steps, 2, hops)),
            dma((steps, chips)),
            dma((steps, chips)),
            dma((steps, chips)),
            dma((steps, chips)),
            dma((steps, 2, hops)),
            dma((steps, 2, hops)),
        ],
        compiler_params=pltpu.CompilerParams(
            collective_id=0, has_side_effects=True, vmem_limit_bytes=64_000_000
        ),
    )(hidden_states, route_ids, route_weights, gate_proj, up_proj, down_proj)


def solution(mesh):
    across = 2 if mesh.shape["groups"] == 2 else 1
    placed = (
        P(None, ("groups", "expert"), None),
        P(None, ("groups", "expert"), None),
        P(None, ("groups", "expert"), None),
        P("expert", None, None),
        P("expert", None, None),
        P("expert", None, None),
    )
    return jax.shard_map(
        functools.partial(on_device, across),
        mesh=mesh,
        in_specs=placed,
        out_specs=P(None, ("groups", "expert"), None),
        check_vma=False,
    )
```

time: 242 us -> 87.4 us (0.36)
  waiting for transfers between devices: 162 us -> 0 us
  Pallas kernels: 0 us -> 82.6 us
  matrix products: 35.1 us -> 0 us
  blocking collectives: 25.4 us -> 0 us
  between operations: 13.1 us -> 0.01 us
  other arithmetic: 3.89 us -> 0 us
    reduce_scatter x2 -> x0, waiting for transfers between devices: 116 us -> none  [on_device(): lax.psum_scatter(partial, 'expert', scatter_dimension=0, tiled=True)]
    pallas_call x0 -> x1, Pallas kernels: none -> 82.6 us  [on_device(): pl.pallas_call(functools.partial(kernel, chips, across), out_shape=jax.Sh...]
    all_gather x2 -> x0, waiting for transfers between devices: 45.5 us -> none  [on_device(): tokens = lax.all_gather(hidden_states[step], 'expert', axis=0, tiled=True)]
    dot_general x4 -> x0, matrix products: 35.1 us -> none  [the longest x2 22.1 us: on_device(): result = jnp.dot(hidden, down_proj[0], preferred_element_type=jnp.float32)]
    all_gather x1 -> x0, blocking collectives: 25.4 us -> none  [on_device(): all_dense = lax.all_gather(dense, 'expert', axis=1, tiled=True)]
    unnamed x6 -> x3, local copies, waits for them, and re-layouts: 0.24 us -> 4.5 us
  transfers between devices with their start and end apart: 4 -> 0, of which waited for: 4 -> 0; matrix products, arithmetic and copies ran while one was open for 16% -> 0% of each run, Pallas kernels for 0% -> 0%
where the time goes in v2:
time: 87.4 us; the launch traced here: 87.1 us
  Pallas kernels  82.6 us (95%)
  local copies, waits for them, and re-layouts  4.5 us (5%)
    pallas_call x1, Pallas kernels, on_device(): pl.pallas_call(functools.partial(kernel, chips, across), out_shape=jax.Sh...  82.6 us
    unnamed x3, local copies, waits for them, and re-layouts  4.5 us

profile of v2, /device:TPU:0, one launch (start us, length us, event | category | flops | bytes accessed | tf_op | source)
XLA Modules:
  0.0 87.1 jit_solution(12007353233508230597)
XLA Ops:
  0.0 1.4 %copy.7.ids_ref = s32[2,32,8]{2,1,0:T(8,128)} copy(s32[2,32,8]{1,2,0:T(8,128)} %param.7) | data formatting | bytes 4096 | tf_op args[1]
  1.4 1.4 %copy.8.weights_ref = f32[2,32,8]{2,1,0:T(8,128)} copy(f32[2,32,8]{1,2,0:T(8,128)} %param.8) | data formatting | bytes 4096 | tf_op args[2]
  2.8 82.6 %shard_map.64 = bf16[2,32,2560]{2,1,0:T(8,128)(2,1)} custom-call(bf16[2,32,2560]{2,1,0:T(8,128)(2,1)} %hidden_ref.1, s32[2,32,8]{2,1,0:T(8,128)} %copy.7.ids_ref, f32[2,32,8]{2,1,0:T(8,128)} %copy.8.weights_ref, bf16[1,2560,768]{2,1,0:T(8,128)(2,1)} %gate_hbm.1, bf16[1,2560,768]{2,1,0:T(8,128)(2,1)} %up_hbm.1, bf16[1,768,2560]{2,1,0:T(8,128)(2,1)} %down_hbm.1), custom_call_target="tpu_custom_call" | custom-call | tf_op jit(solution)/shard_map/pallas_call | solution.py:322
  85.4 1.7 %copy.10 = bf16[2,32,2560]{2,1,0:T(8,128)(2,1)} copy(bf16[2,32,2560]{2,1,0:T(8,128)(2,1)} %shard_map.64) | data formatting | bytes 655360

commit v3 on v2

--- a/solution.py
+++ b/solution.py
@@ -9,6 +9,7 @@
 
 MESH = pl.DeviceIdType.MESH
 LANES = 128
+CUTS = 2
 
 
 def kernel(
@@ -76,6 +77,10 @@
         order += [slot(d, hop) for d in range(2) if hop <= hops[d]]
     place = {s: i for i, s in enumerate(order)}
     values = pl.ds(0, width)
+    cut = rows // CUTS
+
+    def some(q):
+        return pl.ds(q * cut, cut)
 
     def remote(src, dst, send, recv, target):
         return pltpu.make_async_remote_copy(
@@ -90,21 +95,21 @@
     def mirror(s):
         return (chips - s) % chips
 
-    def ag_copy(st, d, hop):
+    def ag_copy(st, d, hop, q):
         return remote(
-            x.at[st, place[slot(d, hop - 1)], 0],
-            x.at[st, place[slot(d, hop)], 0],
-            ag_s.at[st, d, hop - 1],
-            ag_r.at[st, d, hop - 1],
+            x.at[st, place[slot(d, hop - 1)], 0, some(q)],
+            x.at[st, place[slot(d, hop)], 0, some(q)],
+            ag_s.at[st, d, hop - 1, q],
+            ag_r.at[st, d, hop - 1, q],
             neighbours[d],
         )
 
-    def pf_copy(st, s):
+    def pf_copy(st, s, q):
         return remote(
-            x.at[st, place[s], 0],
-            x.at[st, place[mirror(s)], 1],
-            pf_s.at[st, s],
-            pf_r.at[st, mirror(s)],
+            x.at[st, place[s], 0, some(q)],
+            x.at[st, place[mirror(s)], 1, some(q)],
+            pf_s.at[st, s, q],
+            pf_r.at[st, mirror(s), q],
             partner,
         )
 
@@ -117,13 +122,13 @@
             partner,
         )
 
-    def rs_copy(st, d, hop):
+    def rs_copy(st, d, hop, q):
         target = slot(d, hop - 1) if (d == 0 or hop > 1) else chips // 2
         return remote(
-            x.at[st, place[slot(d, hop)], 0, :, values],
-            rs.at[st, target],
-            rs_s.at[st, d, hop - 1],
-            rs_r.at[st, d, hop - 1],
+            x.at[st, place[slot(d, hop)], 0, some(q), values],
+            rs.at[st, target, some(q)],
+            rs_s.at[st, d, hop - 1, q],
+            rs_r.at[st, d, hop - 1, q],
             neighbours[1 - d],
         )
 
@@ -150,8 +155,8 @@
     lane = lax.broadcasted_iota(jnp.int32, (rows, extra), 1)
     for st in range(steps):
         raw = weights_ref[st]
-        normalized = raw / jnp.sum(raw, axis=1, keepdims=True)
-        ids = ids_ref[st]
+        normalized = (raw / jnp.sum(raw, axis=0, keepdims=True)).T
+        ids = ids_ref[st].T
         dense = jnp.zeros((rows, extra), jnp.float32)
         for k in range(ids.shape[1]):
             label = ids[:, k : k + 1]
@@ -166,42 +171,47 @@
 
     def ag_open(st):
         own[st].wait()
-        for d in range(2):
-            ag_copy(st, d, 1).start()
-        pf_copy(st, 0).start()
-
-    def ag_event(st, hop):
+        for q in range(CUTS):
+            for d in range(2):
+                ag_copy(st, d, 1, q).start()
+        for q in range(CUTS):
+            pf_copy(st, 0, q).start()
+
+    def ag_event(st, hop, q):
         for d in range(2):
             if hop <= hops[d]:
-                ag_copy(st, d, hop).wait_recv()
+                ag_copy(st, d, hop, q).wait_recv()
                 if hop < hops[d]:
-                    ag_copy(st, d, hop + 1).start()
-                pf_copy(st, slot(d, hop)).start()
-
-    def total(st, s, received):
-        value = x[st, place[s], 0, :, values].astype(jnp.float32)
-        value = value + pc[st, s].astype(jnp.float32)
+                    ag_copy(st, d, hop + 1, q).start()
+                pf_copy(st, slot(d, hop), q).start()
+
+    def total(st, s, received, q):
+        value = x[st, place[s], 0, some(q), values].astype(jnp.float32)
+        value = value + pc[st, s, some(q)].astype(jnp.float32)
         for index in received:
-            value = value + rs[st, index].astype(jnp.float32)
+            value = value + rs[st, index, some(q)].astype(jnp.float32)
         return value.astype(jnp.bfloat16)
 
-    def rs_event(st, hop):
+    def rs_event(st, age, q):
         for d in range(2):
-            if hop <= hops[d]:
+            hop = hops[d] - age
+            if hop >= 1:
                 s = slot(d, hop)
                 received = []
-                if hop < hops[d]:
-                    rs_copy(st, d, hop + 1).wait_recv()
+                if age:
+                    rs_copy(st, d, hop + 1, q).wait_recv()
                     received = [s]
-                pc_copy(st, mirror(s)).wait_recv()
-                x[st, place[s], 0, :, values] = total(st, s, received)
-                rs_copy(st, d, hop).start()
-
-    def rs_close(st):
+                if q == 0:
+                    pc_copy(st, mirror(s)).wait_recv()
+                x[st, place[s], 0, some(q), values] = total(st, s, received, q)
+                rs_copy(st, d, hop, q).start()
+
+    def rs_close(st, q):
+        if q == 0:
+            pc_copy(st, 0).wait_recv()
         for d in range(2):
-            rs_copy(st, d, 1).wait_recv()
-        pc_copy(st, 0).wait_recv()
-        out_ref[st] = total(st, 0, [0, chips // 2])
+            rs_copy(st, d, 1, q).wait_recv()
+        out_ref[st, some(q)] = total(st, 0, [0, chips // 2], q)
 
     group = chips // 2
     block = min(4, group)
@@ -232,11 +242,12 @@
 
     def down_all(st, part):
         for s in order[part * group : (part + 1) * group]:
-            pf_copy(st, s).wait_send()
-            for d in range(2):
-                for hop in range(hops[d]):
-                    if slot(d, hop) == s:
-                        ag_copy(st, d, hop + 1).wait_send()
+            for q in range(CUTS):
+                pf_copy(st, s, q).wait_send()
+                for d in range(2):
+                    for hop in range(hops[d]):
+                        if slot(d, hop) == s:
+                            ag_copy(st, d, hop + 1, q).wait_send()
 
         def body(first, row):
             marks = x[st, pl.ds(first, block), :, :, pl.ds(width, extra)].reshape(tall, extra)
@@ -262,7 +273,8 @@
 
     def arrive(st, part):
         for s in order[part * group : (part + 1) * group]:
-            pf_copy(st, mirror(s)).wait_recv()
+            for q in range(CUTS):
+                pf_copy(st, mirror(s), q).wait_recv()
 
     def compute(st, part, events):
         tiles = inner // ff_tile
@@ -281,29 +293,44 @@
 
     near = group // 2
     call = functools.partial
+
+    def gathers(st, first, last):
+        return [
+            call(ag_event, st, hop, q) for hop in range(first, last + 1) for q in range(CUTS)
+        ]
+
+    def returns(st, first, last):
+        return [call(rs_event, st, age, q) for age in range(first, last) for q in range(CUTS)]
+
+    def mixed(one, two):
+        keyed = [((i + 1) / len(one), 0, i, e) for i, e in enumerate(one)]
+        keyed += [((i + 1) / len(two), 1, i, e) for i, e in enumerate(two)]
+        return [entry[3] for entry in sorted(keyed, key=lambda entry: entry[:3])]
+
+    far = hops[0]
     ag_open(0)
-    for hop in range(1, near + 1):
-        ag_event(0, hop)
+    for event in gathers(0, 1, near):
+        event()
     for copy in loads:
         copy.wait()
-    rest = [call(ag_event, 0, hop) for hop in range(near + 1, hops[0] + 1)]
-    compute(0, 0, rest + [call(ag_open, 1)])
-    later = [call(ag_event, 1, hop) for hop in range(1, hops[0] + 1)]
-    compute(0, 1, later[:near])
-    back = [call(rs_event, 0, hop) for hop in range(hops[0], 0, -1)]
-    mixed = []
-    for i in range(near):
-        mixed += [back[i]] + later[near + i * (len(later) - near) // near : near + (i + 1) * (len(later) - near) // near]
-    compute(1, 0, mixed)
-    compute(1, 1, back[near:] + [call(rs_close, 0)])
-    for hop in range(hops[0], 0, -1):
-        rs_event(1, hop)
-    rs_close(1)
+    compute(0, 0, gathers(0, near + 1, far - 1) + [call(ag_open, 1)] + gathers(0, far, far))
+    compute(0, 1, gathers(1, 1, near))
+    middle = max(1, far // 2)
+    for event in returns(0, 0, 1):
+        event()
+    compute(1, 0, mixed(gathers(1, near + 1, far), returns(0, 1, middle)))
+    closing = [call(rs_close, 0, q) for q in range(CUTS)]
+    compute(1, 1, returns(0, middle, far))
+    for event in returns(1, 0, 1) + closing + returns(1, 1, far):
+        event()
+    for q in range(CUTS):
+        rs_close(1, q)
 
     for st in range(steps):
         for d in range(2):
             for hop in range(1, hops[d] + 1):
-                rs_copy(st, d, hop).wait_send()
+                for q in range(CUTS):
+                    rs_copy(st, d, hop, q).wait_send()
         for s in range(chips):
             pc_copy(st, s).wait_send()
 
@@ -333,19 +360,19 @@
             pltpu.VMEM((inner, width), bf16),
             pltpu.VMEM((chips * rows, inner), bf16),
             dma((3 + steps,)),
-            dma((steps, 2, hops)),
-            dma((steps, 2, hops)),
+            dma((steps, 2, hops, CUTS)),
+            dma((steps, 2, hops, CUTS)),
+            dma((steps, chips, CUTS)),
+            dma((steps, chips, CUTS)),
             dma((steps, chips)),
             dma((steps, chips)),
-            dma((steps, chips)),
-            dma((steps, chips)),
-            dma((steps, 2, hops)),
-            dma((steps, 2, hops)),
+            dma((steps, 2, hops, CUTS)),
+            dma((steps, 2, hops, CUTS)),
         ],
         compiler_params=pltpu.CompilerParams(
             collective_id=0, has_side_effects=True, vmem_limit_bytes=64_000_000
         ),
-    )(hidden_states, route_ids, route_weights, gate_proj, up_proj, down_proj)
+    )(hidden_states, route_ids.swapaxes(1, 2), route_weights.swapaxes(1, 2), gate_proj, up_proj, down_proj)
 
 
 def solution(mesh):

time: 87.4 us -> 74.1 us (0.85)
  Pallas kernels: 82.6 us -> 72.1 us
  local copies, waits for them, and re-layouts: 4.5 us -> 1.72 us
    pallas_call x1, Pallas kernels: 82.6 us -> 72.1 us  [on_device(): pl.pallas_call(functools.partial(kernel, chips, across), out_shape=jax.Sh...]
    unnamed x3 -> x1, local copies, waits for them, and re-layouts: 4.5 us -> 1.72 us
where the time goes in v3:
time: 74.1 us; the launch traced here: 73.8 us
  Pallas kernels  72.1 us (97%)
  local copies, waits for them, and re-layouts  1.72 us (2%)
    pallas_call x1, Pallas kernels, on_device(): pl.pallas_call(functools.partial(kernel, chips, across), out_shape=jax.Sh...  72.1 us
    unnamed x1, local copies, waits for them, and re-layouts  1.72 us

profile of v3, /device:TPU:0, one launch (start us, length us, event | category | flops | bytes accessed | tf_op | source)
XLA Modules:
  0.0 73.8 jit_solution(13810112874358491672)
XLA Ops:
  0.0 72.1 %shard_map.64 = bf16[2,32,2560]{2,1,0:T(8,128)(2,1)} custom-call(bf16[2,32,2560]{2,1,0:T(8,128)(2,1)} %hidden_ref.1, s32[2,8,32]{2,1,0:T(8,128)} %bitcast.2, f32[2,8,32]{2,1,0:T(8,128)} %bitcast.3, bf16[1,2560,768]{2,1,0:T(8,128)(2,1)} %gate_hbm.1, bf16[1,2560,768]{2,1,0:T(8,128)(2,1)} %up_hbm.1, bf16[1,768,2560]{2,1,0:T(8,128)(2,1)} %down_hbm.1), custom_call_target="tpu_custom_call" | custom-call | tf_op jit(solution)/shard_map/pallas_call | solution.py:349
  72.1 1.7 %copy.8 = bf16[2,32,2560]{2,1,0:T(8,128)(2,1)} copy(bf16[2,32,2560]{2,1,0:T(8,128)(2,1)} %shard_map.64) | data formatting | bytes 655360

commit v4 on v3

--- a/solution.py
+++ b/solution.py
@@ -132,6 +132,10 @@
             neighbours[1 - d],
         )
 
+    barrier = pltpu.get_barrier_semaphore()
+    for target in (*neighbours, partner):
+        pl.semaphore_signal(barrier, inc=1, device_id=target, device_id_type=MESH)
+
     own = [
         pltpu.make_async_copy(
             hidden_ref.at[st], x.at[st, 0, 0, :, values], load_sem.at[3 + st]
@@ -146,10 +150,6 @@
     ]
     for copy in loads:
         copy.start()
-
-    barrier = pltpu.get_barrier_semaphore()
-    for target in (*neighbours, partner):
-        pl.semaphore_signal(barrier, inc=1, device_id=target, device_id_type=MESH)
 
     extra = x.shape[4] - width
     lane = lax.broadcasted_iota(jnp.int32, (rows, extra), 1)
@@ -302,26 +302,26 @@
     def returns(st, first, last):
         return [call(rs_event, st, age, q) for age in range(first, last) for q in range(CUTS)]
 
-    def mixed(one, two):
-        keyed = [((i + 1) / len(one), 0, i, e) for i, e in enumerate(one)]
-        keyed += [((i + 1) / len(two), 1, i, e) for i, e in enumerate(two)]
-        return [entry[3] for entry in sorted(keyed, key=lambda entry: entry[:3])]
-
     far = hops[0]
+    first, second = gathers(0, near + 1, far), gathers(1, 1, far)
+    half = len(first) // 2
     ag_open(0)
     for event in gathers(0, 1, near):
         event()
+    ag_open(1)
     for copy in loads:
         copy.wait()
-    compute(0, 0, gathers(0, near + 1, far - 1) + [call(ag_open, 1)] + gathers(0, far, far))
-    compute(0, 1, gathers(1, 1, near))
+    compute(0, 0, first[:half] + second[:half] + first[half:])
+    compute(0, 1, second[half : 3 * half])
     middle = max(1, far // 2)
     for event in returns(0, 0, 1):
         event()
-    compute(1, 0, mixed(gathers(1, near + 1, far), returns(0, 1, middle)))
+    compute(1, 0, second[3 * half :] + returns(0, 1, middle))
+    compute(1, 1, returns(0, middle, far - 1))
     closing = [call(rs_close, 0, q) for q in range(CUTS)]
-    compute(1, 1, returns(0, middle, far))
-    for event in returns(1, 0, 1) + closing + returns(1, 1, far):
+    for event in returns(1, 0, 1) + returns(0, far - 1, far) + returns(1, 1, 2):
+        event()
+    for event in closing + returns(1, 2, far):
         event()
     for q in range(CUTS):
         rs_close(1, q)

time: 74.1 us -> 71.5 us (0.965)
  Pallas kernels: 72.1 us -> 69.5 us
    pallas_call x1, Pallas kernels: 72.1 us -> 69.5 us  [on_device(): pl.pallas_call(functools.partial(kernel, chips, across), out_shape=jax.Sh...]
where the time goes in v4:
time: 71.5 us; the launch traced here: 71.2 us
  Pallas kernels  69.5 us (97%)
  local copies, waits for them, and re-layouts  1.72 us (2%)
    pallas_call x1, Pallas kernels, on_device(): pl.pallas_call(functools.partial(kernel, chips, across), out_shape=jax.Sh...  69.5 us
    unnamed x1, local copies, waits for them, and re-layouts  1.72 us

profile of v4, /device:TPU:0, one launch (start us, length us, event | category | flops | bytes accessed | tf_op | source)
XLA Modules:
  0.0 71.2 jit_solution(4694384132354632934)
XLA Ops:
  0.0 69.5 %shard_map.64 = bf16[2,32,2560]{2,1,0:T(8,128)(2,1)} custom-call(bf16[2,32,2560]{2,1,0:T(8,128)(2,1)} %hidden_ref.1, s32[2,8,32]{2,1,0:T(8,128)} %bitcast.2, f32[2,8,32]{2,1,0:T(8,128)} %bitcast.3, bf16[1,2560,768]{2,1,0:T(8,128)(2,1)} %gate_hbm.1, bf16[1,2560,768]{2,1,0:T(8,128)(2,1)} %up_hbm.1, bf16[1,768,2560]{2,1,0:T(8,128)(2,1)} %down_hbm.1), custom_call_target="tpu_custom_call" | custom-call | tf_op jit(solution)/shard_map/pallas_call | solution.py:349
  69.5 1.7 %copy.8 = bf16[2,32,2560]{2,1,0:T(8,128)(2,1)} copy(bf16[2,32,2560]{2,1,0:T(8,128)(2,1)} %shard_map.64) | data formatting | bytes 655360
